TPU v7x, 32 devices: a whole 2x2x4 slice. The times are simulated.
32 devices in a mesh: dp: 4 (over x, core), ctx: 8 (over z, y).
Axes of the slice: x: 2, y: 2, z: 4, core: 2. Of those that a mesh axis runs over, the one named last changes fastest.
Arguments:
- tokens: bfloat16 [4, 4096, 512], P('dp', 'ctx'), may hold values from -6 to 6
- piece_starts: int32 [4, 4], P('dp'), may hold values from 0 to 3840, as said below
- qkv_weight: bfloat16 [786432], P(('dp', 'ctx')), may hold values from -0.375 to 0.375
- out_weight: bfloat16 [262144], P(('dp', 'ctx')), may hold values from -0.75 to 0.75
- up_weight: bfloat16 [1048576], P(('dp', 'ctx')), may hold values from -0.25 to 0.25
- down_weight: bfloat16 [1048576], P(('dp', 'ctx')), may hold values from -0.125 to 0.125
- biases: bfloat16 [4096], P(('dp', 'ctx')), may hold values from -2 to 2
- norms: bfloat16 [2048], P(('dp', 'ctx'))
- cotangent: bfloat16 [4, 4096, 512], P('dp', 'ctx'), may hold values from -6 to 6
Outputs:
- output: bfloat16 [4, 4096, 512], P('dp', 'ctx')
- grad_tokens: float32 [4, 4096, 512], P('dp', 'ctx')
- grad_qkv: float32 [786432], P(('dp', 'ctx'))
- grad_out: float32 [262144], P(('dp', 'ctx'))
- grad_up: float32 [1048576], P(('dp', 'ctx'))
- grad_down: float32 [1048576], P(('dp', 'ctx'))
- grad_biases: float32 [4096], P(('dp', 'ctx'))
- grad_norms: float32 [2048], P(('dp', 'ctx'))
Inputs may be any that keep to these rules, and one draw needn't show every extreme that they name: `piece_starts`: each row holds 4 distinct multiples of 256 in increasing order; the first is 0 and the last 3840, so that every sequence opens and closes with a picture piece; a piece covers the 256 words from its start.
All inputs are finite; a program needn't handle non-finite values.
Results may differ from a plain program's by a relative error of at most 0.02.
Values may be sent and summed in bfloat16 or wider, within the bound.
A program may use at most 256 MiB of HBM per device.

v0:
```python
import jax
import jax.numpy as jnp
from jax import lax
from jax.sharding import PartitionSpec as P

HEADS = 8
PIECE = 256
eps_norm = 1e-05
masked_score = -1e30


def layer_norm(values, gain, shift):
    center = jnp.mean(values, axis=-1, keepdims=True)
    offsets = values - center
    spread = jnp.mean(offsets * offsets, axis=-1, keepdims=True)
    return offsets * lax.rsqrt(spread + eps_norm) * gain + shift


def gelu_exact(values):
    return jax.nn.gelu(values, approximate=False)


def piece_flags(positions, starts_row):
    opening = positions // PIECE * PIECE
    return jnp.any(opening[:, None] == starts_row[None, :], axis=1)


def visible(query_pos, query_flag, key_pos):
    causal = key_pos[None, :] <= query_pos[:, None]
    same_piece = key_pos[None, :] // PIECE == query_pos[:, None] // PIECE
    return jnp.logical_or(causal, jnp.logical_and(same_piece, query_flag[:, None]))


def to_blocks(arrays, shard_rows):
    block_len = 256
    block_count = shard_rows // block_len
    shaped = tuple((member.reshape(block_count, block_len, HEADS, -1) for member in arrays))
    return (block_len, block_count, shaped)


def keep_state(state):
    return state


def unpack(flats, model_width):
    qkv_flat, out_flat, up_flat, down_flat, bias_flat, norm_flat = flats
    hidden = up_flat.shape[0] // model_width
    return (
        qkv_flat.reshape(model_width, 3 * model_width),
        out_flat.reshape(model_width, model_width),
        up_flat.reshape(model_width, hidden),
        down_flat.reshape(hidden, model_width),
        bias_flat.astype(jnp.float32),
        norm_flat.astype(jnp.float32),
    )


def norm_back(values, gain, shift, upstream):
    _, pullback = jax.vjp(layer_norm, values, gain, shift)
    return pullback(upstream)


def column_sum(matrix):
    return jnp.sum(matrix.astype(jnp.float32), axis=0)


def query_terms(
    query_heads,
    grad_heads,
    own_lse,
    own_delta,
    query_pos,
    query_flag,
    key_block,
    value_block,
    key_pos,
    factor,
):
    scores = (
        jnp.einsum("qhd,khd->hqk", query_heads, key_block, preferred_element_type=jnp.float32)
        * factor
    )
    allowed = visible(query_pos, query_flag, key_pos)[None]
    softmax_p = jnp.where(allowed, jnp.exp(scores - own_lse[:, :, None]), 0.0)
    dprobs = jnp.einsum("qhd,khd->hqk", grad_heads, value_block, preferred_element_type=jnp.float32)
    dscores = (softmax_p * (dprobs - own_delta[:, :, None])).astype(jnp.bfloat16)
    return (
        jnp.einsum("hqk,khd->hqd", dscores, key_block, preferred_element_type=jnp.float32) * factor
    )


def key_terms(
    query_block,
    grad_block,
    lse_block,
    delta_block,
    remote_pos,
    remote_flag,
    key_heads,
    value_heads,
    key_pos,
    factor,
):
    scores = (
        jnp.einsum("qhd,khd->hqk", query_block, key_heads, preferred_element_type=jnp.float32)
        * factor
    )
    allowed = visible(remote_pos, remote_flag, key_pos)[None]
    softmax_p = jnp.where(allowed, jnp.exp(scores - lse_block[:, :, None]), 0.0)
    dprobs = jnp.einsum("qhd,khd->hqk", grad_block, value_heads, preferred_element_type=jnp.float32)
    dscores = (softmax_p * (dprobs - delta_block[:, :, None])).astype(jnp.bfloat16)
    grad_keys = (
        jnp.einsum("hqk,qhd->hkd", dscores, query_block, preferred_element_type=jnp.float32)
        * factor
    )
    grad_values = jnp.einsum(
        "hqk,qhd->hkd",
        softmax_p.astype(jnp.bfloat16),
        grad_block,
        preferred_element_type=jnp.float32,
    )
    return (grad_keys, grad_values)


def per_device(
    tokens, piece_starts, qkv_weight, out_weight, up_weight, down_weight, biases, norms, cotangent
):
    model_width = tokens.shape[2]
    seq_rows = tokens.shape[1]
    params = unpack(
        (
            lax.all_gather(qkv_weight, ("dp", "ctx"), axis=0, tiled=True),
            lax.all_gather(out_weight, ("dp", "ctx"), axis=0, tiled=True),
            lax.all_gather(up_weight, ("dp", "ctx"), axis=0, tiled=True),
            lax.all_gather(down_weight, ("dp", "ctx"), axis=0, tiled=True),
            lax.all_gather(biases, ("dp", "ctx"), axis=0, tiled=True),
            lax.all_gather(norms, ("dp", "ctx"), axis=0, tiled=True),
        ),
        model_width,
    )
    qkv_mat, out_mat, up_mat, down_mat, bias_all, norm_all = params
    hidden = up_mat.shape[1]
    head_dim = model_width // HEADS
    factor = head_dim ** (-0.5)
    first_row = lax.axis_index("ctx") * seq_rows
    last_row = first_row + seq_rows - 1
    query_pos = first_row + jnp.arange(seq_rows, dtype=jnp.int32)
    starts_row = piece_starts[0]
    query_flag = piece_flags(query_pos, starts_row)
    bias_q = bias_all[:model_width]
    bias_v = bias_all[model_width : 2 * model_width]
    bias_o = bias_all[2 * model_width : 3 * model_width]
    bias_up = bias_all[3 * model_width : 3 * model_width + hidden]
    bias_down = bias_all[3 * model_width + hidden :]
    gain_one = norm_all[:model_width]
    shift_one = norm_all[model_width : 2 * model_width]
    gain_two = norm_all[2 * model_width : 3 * model_width]
    shift_two = norm_all[3 * model_width :]
    inputs = tokens[0].astype(jnp.float32)
    first_in = layer_norm(inputs, gain_one, shift_one).astype(jnp.bfloat16)
    projected = jnp.dot(first_in, qkv_mat, preferred_element_type=jnp.float32)
    queries = (projected[:, :model_width] + bias_q).astype(jnp.bfloat16)
    key_rows = projected[:, model_width : 2 * model_width].astype(jnp.bfloat16)
    value_rows = (projected[:, 2 * model_width :] + bias_v).astype(jnp.bfloat16)
    query_heads = queries.reshape(seq_rows, HEADS, head_dim)
    key_heads = key_rows.reshape(seq_rows, HEADS, head_dim)
    value_heads = value_rows.reshape(seq_rows, HEADS, head_dim)
    start_state = (
        jnp.full((HEADS, seq_rows), masked_score, jnp.float32),
        jnp.zeros((HEADS, seq_rows), jnp.float32),
        jnp.zeros((HEADS, seq_rows, head_dim), jnp.float32),
    )
    shard = (
        lax.all_gather(key_rows, "ctx", axis=0, tiled=True),
        lax.all_gather(value_rows, "ctx", axis=0, tiled=True),
    )
    shard_rows = shard[0].shape[0]
    block_len, block_count, (key_blocks, value_blocks) = to_blocks(shard, shard_rows)

    def forward_one_block(state, block_in):
        running_max, running_sum, running_acc = state
        key_block, value_block, position = block_in
        key_pos = position * block_len + jnp.arange(block_len, dtype=jnp.int32)
        scores = (
            jnp.einsum("qhd,khd->hqk", query_heads, key_block, preferred_element_type=jnp.float32)
            * factor
        )
        allowed = visible(query_pos, query_flag, key_pos)[None]
        scores = jnp.where(allowed, scores, masked_score)
        new_max = jnp.maximum(running_max, jnp.max(scores, axis=-1))
        correction = jnp.exp(running_max - new_max)
        exp_scores = jnp.where(allowed, jnp.exp(scores - new_max[:, :, None]), 0.0)
        running_sum = running_sum * correction + jnp.sum(exp_scores, axis=-1)
        running_acc = running_acc * correction[:, :, None] + jnp.einsum(
            "hqk,khd->hqd",
            exp_scores.astype(jnp.bfloat16),
            value_block,
            preferred_element_type=jnp.float32,
        )
        return ((new_max, running_sum, running_acc), None)

    def forward_compute(state):
        return lax.scan(
            forward_one_block,
            state,
            (key_blocks, value_blocks, jnp.arange(block_count, dtype=jnp.int32)),
        )[0]

    run_max, run_sum, run_acc = lax.cond(
        jnp.int32(0) <= last_row, forward_compute, keep_state, start_state
    )
    mixed_heads = run_acc / run_sum[:, :, None]
    mixed_f = jnp.transpose(mixed_heads, (1, 0, 2)).reshape(seq_rows, model_width)
    mixed_b = mixed_f.astype(jnp.bfloat16)
    log_sum = run_max + jnp.log(run_sum)
    after_attn = inputs + jnp.dot(mixed_b, out_mat, preferred_element_type=jnp.float32) + bias_o
    second_in = layer_norm(after_attn, gain_two, shift_two).astype(jnp.bfloat16)
    pre_act = jnp.dot(second_in, up_mat, preferred_element_type=jnp.float32) + bias_up
    activated = gelu_exact(pre_act).astype(jnp.bfloat16)
    result = (
        after_attn + jnp.dot(activated, down_mat, preferred_element_type=jnp.float32) + bias_down
    )
    output = result.astype(jnp.bfloat16)[None]
    back = unpack(
        (
            lax.all_gather(qkv_weight, ("dp", "ctx"), axis=0, tiled=True),
            lax.all_gather(out_weight, ("dp", "ctx"), axis=0, tiled=True),
            lax.all_gather(up_weight, ("dp", "ctx"), axis=0, tiled=True),
            lax.all_gather(down_weight, ("dp", "ctx"), axis=0, tiled=True),
            lax.all_gather(biases, ("dp", "ctx"), axis=0, tiled=True),
            lax.all_gather(norms, ("dp", "ctx"), axis=0, tiled=True),
        ),
        model_width,
    )
    qkv_back, out_back, up_back, down_back, bias_back, norm_vec = back
    gain_one_b = norm_vec[:model_width]
    shift_one_b = norm_vec[model_width : 2 * model_width]
    gain_two_b = norm_vec[2 * model_width : 3 * model_width]
    shift_two_b = norm_vec[3 * model_width :]
    upstream = cotangent[0].astype(jnp.float32)
    grad_mlp = upstream.astype(jnp.bfloat16)
    grad_down_loc = jnp.einsum("ta,tb->ab", activated, grad_mlp, preferred_element_type=jnp.float32)
    grad_act = jnp.einsum("tb,ab->ta", grad_mlp, down_back, preferred_element_type=jnp.float32)
    _, gelu_pull = jax.vjp(gelu_exact, pre_act)
    grad_pre = gelu_pull(grad_act)[0].astype(jnp.bfloat16)
    grad_up_loc = jnp.einsum("ta,tb->ab", second_in, grad_pre, preferred_element_type=jnp.float32)
    grad_second = jnp.einsum("tb,ab->ta", grad_pre, up_back, preferred_element_type=jnp.float32)
    grad_after_part, grad_gain_two, grad_shift_two = norm_back(
        after_attn, gain_two_b, shift_two_b, grad_second
    )
    grad_after = upstream + grad_after_part
    grad_attn = grad_after.astype(jnp.bfloat16)
    grad_out_loc = jnp.einsum("ta,tb->ab", mixed_b, grad_attn, preferred_element_type=jnp.float32)
    grad_mixed = jnp.einsum(
        "tb,ab->ta", grad_attn, out_back, preferred_element_type=jnp.float32
    ).astype(jnp.bfloat16)
    grad_heads = grad_mixed.reshape(seq_rows, HEADS, head_dim)
    delta_rows = jnp.sum(
        grad_heads.astype(jnp.float32) * mixed_f.reshape(seq_rows, HEADS, head_dim), axis=-1
    )
    delta_heads = delta_rows.T
    stats = jnp.concatenate([log_sum.T, delta_rows], axis=1)
    all_stats = lax.all_gather(stats, "ctx", axis=0, tiled=True)
    zero_heads = jnp.zeros((HEADS, seq_rows, head_dim), jnp.float32)
    shard = (
        lax.all_gather(key_rows, "ctx", axis=0, tiled=True),
        lax.all_gather(value_rows, "ctx", axis=0, tiled=True),
    )
    shard_rows = shard[0].shape[0]
    query_block_len, query_block_count, (query_key_blocks, query_value_blocks) = to_blocks(
        shard, shard_rows
    )

    def query_one_block(total, block_in):
        key_block, value_block, position = block_in
        key_pos = position * query_block_len + jnp.arange(query_block_len, dtype=jnp.int32)
        term = query_terms(
            query_heads,
            grad_heads,
            log_sum,
            delta_heads,
            query_pos,
            query_flag,
            key_block,
            value_block,
            key_pos,
            factor,
        )
        return (total + term, None)

    def query_compute(total):
        return lax.scan(
            query_one_block,
            total,
            (query_key_blocks, query_value_blocks, jnp.arange(query_block_count, dtype=jnp.int32)),
        )[0]

    grad_q = lax.cond(jnp.int32(0) <= last_row, query_compute, keep_state, zero_heads)
    shard = (
        lax.all_gather(queries, "ctx", axis=0, tiled=True),
        lax.all_gather(grad_mixed, "ctx", axis=0, tiled=True),
    )
    shard_rows = shard[0].shape[0]
    key_block_len, key_block_count, (query_blocks, grad_blocks) = to_blocks(shard, shard_rows)

    def key_one_block(totals, block_in):
        query_block, grad_block, position = block_in
        begin = position * key_block_len
        remote_pos = begin + jnp.arange(key_block_len, dtype=jnp.int32)
        remote_flag = piece_flags(remote_pos, starts_row)
        stats_block = lax.dynamic_slice_in_dim(all_stats, begin, key_block_len, 0)
        lse_block = stats_block[:, :HEADS].T
        delta_block = stats_block[:, HEADS:].T
        grad_keys, grad_values = key_terms(
            query_block,
            grad_block,
            lse_block,
            delta_block,
            remote_pos,
            remote_flag,
            key_heads,
            value_heads,
            query_pos,
            factor,
        )
        return ((totals[0] + grad_keys, totals[1] + grad_values), None)

    def key_compute(totals):
        return lax.scan(
            key_one_block,
            totals,
            (query_blocks, grad_blocks, jnp.arange(key_block_count, dtype=jnp.int32)),
        )[0]

    grad_k, grad_v = lax.cond(
        jnp.int32(0) + shard_rows - 1 >= first_row,
        key_compute,
        keep_state,
        (zero_heads, zero_heads),
    )

    def merge_heads(grad_part):
        return (
            jnp.transpose(grad_part, (1, 0, 2)).reshape(seq_rows, model_width).astype(jnp.bfloat16)
        )

    grad_qkv_rows = jnp.concatenate(
        [merge_heads(grad_q), merge_heads(grad_k), merge_heads(grad_v)], axis=1
    )
    grad_qkv_loc = jnp.einsum(
        "ta,tb->ab", first_in, grad_qkv_rows, preferred_element_type=jnp.float32
    )
    grad_first = jnp.einsum(
        "tb,ab->ta", grad_qkv_rows, qkv_back, preferred_element_type=jnp.float32
    )
    grad_in_part, grad_gain_one, grad_shift_one = norm_back(
        inputs, gain_one_b, shift_one_b, grad_first
    )
    grad_tokens = (grad_after + grad_in_part)[None]
    grad_bias_loc = jnp.concatenate(
        [
            column_sum(grad_qkv_rows[:, :model_width]),
            column_sum(grad_qkv_rows[:, 2 * model_width :]),
            column_sum(grad_attn),
            column_sum(grad_pre),
            column_sum(grad_mlp),
        ]
    )
    grad_norm_loc = jnp.concatenate([grad_gain_one, grad_shift_one, grad_gain_two, grad_shift_two])
    summed = (
        lax.psum_scatter(grad_qkv_loc.reshape(-1), ("dp", "ctx"), scatter_dimension=0, tiled=True),
        lax.psum_scatter(grad_out_loc.reshape(-1), ("dp", "ctx"), scatter_dimension=0, tiled=True),
        lax.psum_scatter(grad_up_loc.reshape(-1), ("dp", "ctx"), scatter_dimension=0, tiled=True),
        lax.psum_scatter(grad_down_loc.reshape(-1), ("dp", "ctx"), scatter_dimension=0, tiled=True),
        lax.psum_scatter(grad_bias_loc, ("dp", "ctx"), scatter_dimension=0, tiled=True),
        lax.psum_scatter(grad_norm_loc, ("dp", "ctx"), scatter_dimension=0, tiled=True),
    )
    return (output, grad_tokens, summed[0], summed[1], summed[2], summed[3], summed[4], summed[5])


def solution(mesh):
    in_specs = (
        P("dp", "ctx", None),
        P("dp", None),
        P(("dp", "ctx")),
        P(("dp", "ctx")),
        P(("dp", "ctx")),
        P(("dp", "ctx")),
        P(("dp", "ctx")),
        P(("dp", "ctx")),
        P("dp", "ctx", None),
    )
    out_specs = (
        P("dp", "ctx", None),
        P("dp", "ctx", None),
        P(("dp", "ctx")),
        P(("dp", "ctx")),
        P(("dp", "ctx")),
        P(("dp", "ctx")),
        P(("dp", "ctx")),
        P(("dp", "ctx")),
    )
    return jax.shard_map(
        per_device, mesh=mesh, in_specs=in_specs, out_specs=out_specs, check_vma=False
    )
```

profile of v0, /device:TPU:0, one launch (start us, length us, event | category | flops | bytes accessed | tf_op | source)
XLA Modules:
  0.0 1414.8 jit_solution(3792771017945107225)
XLA Ops:
  11.6 42.1 %all-reduce = bf16[2048]{0:T(1024)(128)(2,1)S(1)} all-reduce(bf16[2048]{0:T(1024)(128)(2,1)S(1)} %dynamic-update-slice), channel_id=1, replica_groups=mesh['dp'=4,'ctx'=8] {'dp','ctx'}, use_global_device_ids=true, to_apply=%add | all-reduce | flops 2048 | bytes 8192
  53.7 65.8 %all-gather = bf16[32,1,128]{2,1,0:T(2,128)(2,1)S(1)} all-gather(bf16[1,1,128]{2,1,0:T(2,128)(2,1)} %bitcast.300), channel_id=1, replica_groups=mesh['dp'=4,'ctx'=8] {'dp','ctx'}, dimensions={0}, use_global_device_ids=true | all-gather | bytes 8448 | tf_op jit(solution)/shard_map/all_gather | solution.py:136
  131.3 67.8 %all_gather.45 = bf16[262144]{0:T(1024)(128)(2,1)S(1)} all-gather(bf16[8192]{0:T(1024)(128)(2,1)S(1)} %copy-done.33), channel_id=1, replica_groups=mesh['dp'=4,'ctx'=8] {'dp','ctx'}, dimensions={0}, use_global_device_ids=true | all-gather | bytes 540672 | tf_op jit(solution)/shard_map/all_gather | solution.py:133
  210.1 50.6 %all-gather.13.cloned.1.call-done = bf16[4096,512]{1,0:T(8,128)(2,1)} async-done(((bf16[512,512]{1,0:T(8,128)(2,1)}), bf16[4096,512]{1,0:T(8,128)(2,1)}) %all-gather.13.cloned.1.call-update) | async-done | bytes 4194320 | tf_op jit(solution)/shard_map/all_gather | solution.py:175
  260.7 6.4 copy.89
  267.1 5.8 copy.112
  272.9 62.1 %all-gather.11.cloned.1.call-done = bf16[4096,512]{1,0:T(8,128)(2,1)} async-done(((bf16[512,512]{1,0:T(8,128)(2,1)}), bf16[4096,512]{1,0:T(8,128)(2,1)}) %all-gather.11.cloned.1.call-update) | async-done | bytes 4194320 | tf_op jit(solution)/shard_map/all_gather | solution.py:174
  334.9 6.4 copy.87
  347.4 248.7 %conditional.3 = (f32[8,512]{1,0:T(8,128)}, f32[8,512]{1,0:T(8,128)}, f32[8,512,64]{1,2,0:T(8,128)}, f32[8,512]{1,0:T(8,128)S(1)}) conditional(s32[]{:T(128)} %convert_element_type.146, () %tuple.77, (s32[512]{0:T(512)S(1)}, pred[512]{0:T(512)(128)(4,1)S(1)}, bf16[16,256,8,64]{1,0,3,2:T(8,128)(2,1)S(1)}, bf16[512,8,64]{0,2,1:T(8,128)(2,1)S(1)}, ...), branch_computations={%region_3.4_spmd, %region_4.9_spmd} | conditional | flops 283409920 | bytes 50127792 | solution.py:209
  354.3 241.1 %while.45 = (s32[]{:T(128)}, f32[8,512]{1,0:T(8,128)}, f32[8,512]{1,0:T(8,128)}, f32[8,512,64]{1,2,0:T(8,128)}, s32[16]{0:T(128)S(1)}, /*index=5*/s32[512]{0:T(5...) while((s32[]{:T(128)}, f32[8,512]{1,0:T(8,128)}, ...), condition=%wide.region_8.8_spmd.clone, body=%wide.region_5.7_spmd.clone.sunk | while | flops 283408896 | bytes 33311440 | solution.py:203
  599.4 11.5 multiply_convert_fusion.1
  641.5 181.9 %conditional.4 = (f32[8,512,64]{1,2,0:T(8,128)}) conditional(s32[]{:T(128)} %convert_element_type.146, () %tuple.79, (s32[512]{0:T(512)S(1)}, pred[512]{0:T(512)(128)(4,1)S(1)}, bf16[16,256,8,64]{1,0,3,2:T(8,128)(2,1)}, bf16[512,8,64]{0,2,1:T(8,128)(2,1)S(1)}, f32[8,512]{1,0:T(8,128)S(1)}, /*index=5*/bf16[16,256,8,64]{1,0,3,2:T(8,128)(2,1)}, ...), branch_computations={%region_14.15_spmd, %region_15.18_spmd} | conditional | flops 410267136 | bytes 46196136 | solution.py:298
  641.5 5.8 copy.95
  650.7 172.7 %while.46 = (s32[]{:T(128)}, f32[8,512,64]{1,2,0:T(8,128)}, s32[16]{0:T(128)S(1)}, s32[512]{0:T(512)S(1)}, s32[512,1]{0,1:T(1,128)S(1)}, /*index=5*/s32[512,1]{0...) while((s32[]{:T(128)}, f32[8,512,64]{1,2,0:T(8,128)}, ...), condition=%wide.region_17.17_spmd.clone, body=%wide.region_16.16_spmd.clone.sunk | while | flops 410266112 | bytes 12635323 | solution.py:292
  823.4 30.9 %all_gather.50 = f32[4096,16]{0,1:T(8,128)S(1)} all-gather(f32[512,16]{0,1:T(8,128)S(1)} %pad_maximum_fusion.3), channel_id=1, replica_groups=mesh['dp'=4,'ctx'=8] {'ctx'}, dimensions={0}, use_global_device_ids=true | all-gather | bytes 294912 | tf_op jit(solution)/shard_map/all_gather | solution.py:263
  857.0 304.2 %conditional.5 = (f32[8,512,64]{1,2,0:T(8,128)}, bf16[8,512,64]{1,2,0:T(8,128)(2,1)}, f32[512]{0:T(512)S(1)}) conditional(s32[]{:T(128)} %convert_element_type.166, () %tuple.81, (bf16[4096,512]{1,0:T(8,128)(2,1)}, bf16[4096,512]{0,1:T(8,128)(2,1)}, bf16[512,512]{1,0:T(8,128)(2,1)}, bf16[512,512]{1,0:T(8,128)(2,1)}, s32[512]{0:T(512)S(1)}, ...), branch_computations={%region_18.19_spmd, %region_19.23_spmd} | conditional | flops 549995520 | bytes 56584196 | solution.py:335
  857.6 11.2 reshape.730
  868.8 9.1 copy.84
  888.9 271.4 %while.47 = (s32[]{:T(128)}, f32[8,512,64]{1,2,0:T(8,128)}, f32[8,512,64]{1,2,0:T(8,128)S(1)}, s32[512]{0:T(512)S(1)}, s32[16]{0:T(128)}, /*index=5*/s32[1,512]{...) while((s32[]{:T(128)}, f32[8,512,64]{1,2,0:T(8,128)}, ...), condition=%wide.region_22.22_spmd.clone, body=%wide.region_20.21_spmd.clone.sunk | while | flops 549208576 | bytes 19347220 | solution.py:329
  916.8 5.7 fusion.196
  933.8 5.7 fusion.196
  950.8 5.7 fusion.196
  984.7 5.7 fusion.196
  1018.7 5.7 fusion.196
  1052.7 5.7 fusion.196
  1069.6 5.7 fusion.196
  1086.6 5.7 fusion.196
  1120.6 5.7 fusion.196
  1137.6 5.7 fusion.196
  1154.6 5.7 fusion.196
  1186.7 38.7 %all-reduce.7 = (f32[4096]{0:T(1024)S(1)}, f32[2048]{0:T(1024)S(1)}) all-reduce(f32[4096]{0:T(1024)S(1)} %constant_dynamic-update-slice_fusion, f32[2048]{0:T(1024)S(1)} %pad_maximum_fusion.4), channel_id=6, replica_groups=mesh['dp'=4,'ctx'=8] {'dp','ctx'}, use_global_device_ids=true, to_apply=%region_34.35.clone | all-reduce | flops 6144 | bytes 49152
  1226.6 175.1 %all-reduce.11.cloned.1.call-done = (f32[786432]{0:T(1024)}, f32[262144]{0:T(1024)}, f32[1048576]{0:T(1024)}, f32[1048576]{0:T(1024)}) async-done(((f32[786432]{0:T(1024)}, f32[262144]{0:T(1024)}, f32[1048576]{0:T(1024)}, f32[1048576]{0:T(1024)}), (f32[786432]{0:T(1024)}, f32[262144]{0:T(1024)}, f32[1048576]{0:T(1024)}, f32[1048576]{0:T(1024)})) %all-reduce.11.cloned.1.call-update) | async-done | bytes 12582928
  (685 shorter events, 714.7 us)
Async XLA Ops:
  7.2 113.8 %all-gather.9.cloned.1.call-start = ((), (), s32[]{:S(2)}) async-start(), calls=%async_computation | async-start | bytes 1622016 | tf_op jit(solution)/shard_map/all_gather | solution.py:132
  7.9 193.6 %all-gather.15.cloned.1.call-start = ((), (), s32[]{:S(2)}) async-start(), calls=%async_computation.3 | async-start | bytes 2162688 | tf_op jit(solution)/shard_map/all_gather | solution.py:134
  8.7 197.1 %all-gather.17.cloned.1.call-start = ((), (), s32[]{:S(2)}) async-start(), calls=%async_computation.4 | async-start | bytes 2162688 | tf_op jit(solution)/shard_map/all_gather | solution.py:135
  9.4 251.3 %all-gather.13.cloned.1.call-start = ((), (), s32[]{:S(2)}) async-start(), calls=%async_computation.2 | async-start | bytes 4718592 | tf_op jit(solution)/shard_map/all_gather | solution.py:175
  125.4 5.9 copy-start.33
  125.4 74.8 %copy-start.19 = (bf16[1,512,512]{2,1,0:T(8,128)(2,1)S(1)}, bf16[1,512,512]{2,1,0:T(8,128)(2,1)}, u32[]{:S(2)}) copy-start(bf16[1,512,512]{2,1,0:T(8,128)(2,1)} %param.29) | copy-start | bytes 1572868
  128.4 72.8 %copy-start.9 = (bf16[512,512]{1,0:T(8,128)(2,1)S(1)}, bf16[512,512]{1,0:T(8,128)(2,1)}, u32[]{:S(2)}) copy-start(bf16[512,512]{1,0:T(8,128)(2,1)} %get-tuple-element.1027) | copy-start | bytes 1572868
  128.4 206.5 %all-gather.11.cloned.1.call-start = ((), (), s32[]{:S(2)}) async-start(), calls=%async_computation.1 | async-start | bytes 4718592 | tf_op jit(solution)/shard_map/all_gather | solution.py:174
  130.6 726.4 %all-gather.19.cloned.1.call-start = ((), (), s32[]{:S(2)}) async-start(), calls=%async_computation.5 | async-start | bytes 4718592 | tf_op jit(solution)/shard_map/all_gather | solution.py:300
  131.2 725.8 %all-gather.21.cloned.1.call-start = ((), (), s32[]{:S(2)}) async-start(), calls=%async_computation.6 | async-start | bytes 4718592 | tf_op jit(solution)/shard_map/all_gather | solution.py:301
  200.4 423.5 %copy-start.6 = (bf16[1,512,512]{1,2,0:T(8,128)(2,1)}, bf16[1,512,512]{1,2,0:T(8,128)(2,1)S(1)}, u32[]{:S(2)}) copy-start(bf16[1,512,512]{1,2,0:T(8,128)(2,1)S(1)} %copy.93) | copy-start | bytes 1572868
  372.7 5.7 copy-start
  388.0 5.7 copy-start
  403.2 5.6 copy-start
  418.4 5.6 copy-start
  433.5 5.6 copy-start
  448.7 5.6 copy-start
  463.9 5.6 copy-start
  479.1 5.6 copy-start
  494.2 5.6 copy-start
  509.4 5.6 copy-start
  524.6 5.6 copy-start
  539.8 5.6 copy-start
  554.9 5.6 copy-start
  570.1 5.6 copy-start
  585.3 5.6 copy-start
  599.4 11.6 copy-start.13
  599.4 11.6 copy-start.20
  624.0 7.5 copy-start.30
  628.4 773.2 %all-reduce.11.cloned.1.call-start = ((), (), s32[]{:S(2)}) async-start(), calls=%async_computation.7 | async-start | bytes 25165824
  641.5 5.8 copy-start.2
  1176.4 5.6 copy-start.27
  (34 other events, 117.9 us)
Sparse Core Ops, SparseCore 0:
  10.9 57.8 all-gather.8
  71.7 55.3 all-gather.14
  130.2 56.0 all-gather.16
  188.3 72.3 all-gather.12
  263.2 71.6 all-gather.10
  336.9 71.6 all-gather.18
  628.6 73.0 all-gather.20
  1171.2 230.4 all-reduce.10
where the time goes:
time: 1430 us; the launch traced here: 1410 us
  matrix products  510 us (36%)
  waiting for transfers between devices  290 us (20%)
  blocking collectives  245 us (17%)
  local copies, waits for them, and re-layouts  180 us (13%)
  other arithmetic  141 us (10%)
  loops' own time  33 us (2%)
  between operations  15 us (1%)
    unnamed x9, waiting for transfers between devices  178 us
    dot_general x16, matrix products, key_terms(): jnp.einsum('hqk,qhd->hkd', dscores, query_block, preferred_element_type=j...  91 us
    dot_general x16, matrix products, query_terms(): jnp.einsum('hqk,khd->hqd', dscores, key_block, preferred_element_type=jnp...  88 us
    unnamed x2, blocking collectives  80.8 us
    all_gather x1, blocking collectives, per_device(): lax.all_gather(out_weight, ('dp', 'ctx'), axis=0, tiled=True)  67.8 us
    all_gather x1, blocking collectives, per_device(): lax.all_gather(biases, ('dp', 'ctx'), axis=0, tiled=True)  65.8 us
    all_gather x1, waiting for transfers between devices, per_device(): lax.all_gather(key_rows, 'ctx', axis=0, tiled=True)  62.1 us
    dot_general x16, matrix products, query_terms(): jnp.einsum('qhd,khd->hqk', query_heads, key_block, preferred_element_type...  60.4 us
  transfers between devices with their start and end apart: 8, of which 3 were waited for; matrix products, arithmetic and copies ran while one was open for 36% of the time, Pallas kernels for 0%

commit v1 on v0

--- a/solution.py
+++ b/solution.py
@@ -7,6 +7,25 @@
 PIECE = 256
 eps_norm = 1e-05
 masked_score = -1e30
+
+
+def ring_gather(array, axis, dim):
+    size, here, rows = (lax.axis_size(axis), lax.axis_index(axis), array.shape[dim])
+    ahead = [(i, (i + 1) % size) for i in range(size)]
+    left = [(i, (i - 1) % size) for i in range(size)]
+    out = jnp.zeros((*array.shape[:dim], size * rows, *array.shape[dim + 1 :]), array.dtype)
+    out = lax.dynamic_update_slice_in_dim(out, array, here * rows, axis=dim)
+    from_left = from_right = array
+    half = size // 2
+    for step in range(1, half + 1):
+        from_left = lax.ppermute(from_left, axis, ahead)
+        out = lax.dynamic_update_slice_in_dim(out, from_left, (here - step) % size * rows, axis=dim)
+        if step < size - half:
+            from_right = lax.ppermute(from_right, axis, left)
+            out = lax.dynamic_update_slice_in_dim(
+                out, from_right, (here + step) % size * rows, axis=dim
+            )
+    return out
 
 
 def layer_norm(values, gain, shift):
@@ -170,10 +189,7 @@
         jnp.zeros((HEADS, seq_rows), jnp.float32),
         jnp.zeros((HEADS, seq_rows, head_dim), jnp.float32),
     )
-    shard = (
-        lax.all_gather(key_rows, "ctx", axis=0, tiled=True),
-        lax.all_gather(value_rows, "ctx", axis=0, tiled=True),
-    )
+    shard = (ring_gather(key_rows, "ctx", 0), lax.all_gather(value_rows, "ctx", axis=0, tiled=True))
     shard_rows = shard[0].shape[0]
     block_len, block_count, (key_blocks, value_blocks) = to_blocks(shard, shard_rows)
 

time: 1430 us -> 1430 us (level)
  waiting for transfers between devices: 290 us -> 234 us
  local copies, waits for them, and re-layouts: 180 us -> 211 us
  starting transfers between devices: 0.31 us -> 17.1 us
    all_gather x1, waiting for transfers between devices: 62.1 us -> 0.01 us  [per_device(): lax.all_gather(key_rows, 'ctx', axis=0, tiled=True)]
    ppermute x0 -> x7, waiting for transfers between devices: none -> 56.1 us  [the longest x4 56 us: ring_gather(): from_left = lax.ppermute(from_left, axis, ahead)]
    all_gather x1, waiting for transfers between devices: 50.6 us -> 0.01 us  [per_device(): lax.all_gather(value_rows, 'ctx', axis=0, tiled=True)]
    ppermute x0 -> x7, starting transfers between devices: none -> 16.7 us  [the longest x3 9.24 us: ring_gather(): from_right = lax.ppermute(from_right, axis, left)]
    cond x5 -> x10, local copies, waits for them, and re-layouts: 16.2 us -> 32.3 us
    unnamed x103 -> x104, local copies, waits for them, and re-layouts: 36.4 us -> 31.3 us
  transfers between devices with their start and end apart: 8 -> 15, of which waited for: 3 -> 5; matrix products, arithmetic and copies ran while one was open for 36% -> 39% of each run, Pallas kernels for 0% -> 0%
where the time goes in v1:
time: 1430 us; the launch traced here: 1420 us
  matrix products  511 us (36%)
  blocking collectives  256 us (18%)
  waiting for transfers between devices  234 us (16%)
  local copies, waits for them, and re-layouts  211 us (15%)
  other arithmetic  140 us (10%)
  loops' own time  33.6 us (2%)
  starting transfers between devices  17.1 us (1%)
  between operations  15 us (1%)
    unnamed x9, waiting for transfers between devices  178 us
    dot_general x16, matrix products, key_terms(): jnp.einsum('hqk,qhd->hkd', dscores, query_block, preferred_element_type=j...  91.1 us
    dot_general x16, matrix products, query_terms(): jnp.einsum('hqk,khd->hqd', dscores, key_block, preferred_element_type=jnp...  89.9 us
    unnamed x2, blocking collectives  81.2 us
    all_gather x1, blocking collectives, per_device(): lax.all_gather(out_weight, ('dp', 'ctx'), axis=0, tiled=True)  78.6 us
    all_gather x1, blocking collectives, per_device(): lax.all_gather(biases, ('dp', 'ctx'), axis=0, tiled=True)  65.8 us
    dot_general x16, matrix products, forward_one_block(): jnp.einsum('qhd,khd->hqk', query_heads, key_block, preferred_element_type...  61 us
    dot_general x16, matrix products, query_terms(): jnp.einsum('qhd,khd->hqk', query_heads, key_block, preferred_element_type...  59.8 us
  transfers between devices with their start and end apart: 15, of which 5 were waited for; matrix products, arithmetic and copies ran while one was open for 39% of the time, Pallas kernels for 0%

profile of v1, /device:TPU:0, one launch (start us, length us, event | category | flops | bytes accessed | tf_op | source)
XLA Modules:
  0.0 1419.4 jit_solution(5526134584638196509)
XLA Ops:
  11.6 42.1 %all-reduce = bf16[2048]{0:T(1024)(128)(2,1)S(1)} all-reduce(bf16[2048]{0:T(1024)(128)(2,1)S(1)} %dynamic-update-slice), channel_id=1, replica_groups=mesh['dp'=4,'ctx'=8] {'dp','ctx'}, use_global_device_ids=true, to_apply=%add | all-reduce | flops 2048 | bytes 8192
  53.7 65.8 %all-gather = bf16[32,1,128]{2,1,0:T(2,128)(2,1)S(1)} all-gather(bf16[1,1,128]{2,1,0:T(2,128)(2,1)} %bitcast.301), channel_id=1, replica_groups=mesh['dp'=4,'ctx'=8] {'dp','ctx'}, dimensions={0}, use_global_device_ids=true | all-gather | bytes 8448 | tf_op jit(solution)/shard_map/all_gather | solution.py:155
  135.4 12.9 collective-permute-done
  153.1 20.3 %collective-permute-done.2 = bf16[512,512]{1,0:T(8,128)(2,1)S(1)} collective-permute-done((bf16[512,512]{1,0:T(8,128)(2,1)S(1)}, bf16[512,512]{1,0:T(8,128)(2,1)S(1)}, u32[]{:S(2)}, u32[]{:S(2)}) %collective-permute-start.2) | collective-permute-done | bytes 524320 | tf_op jit(solution)/shard_map/ppermute | solution.py:21
  178.2 22.8 %collective-permute-done.4 = bf16[512,512]{1,0:T(8,128)(2,1)} collective-permute-done((bf16[512,512]{1,0:T(8,128)(2,1)S(1)}, bf16[512,512]{1,0:T(8,128)(2,1)}, u32[]{:S(2)}, u32[]{:S(2)}) %collective-permute-start.4) | collective-permute-done | bytes 524320 | tf_op jit(solution)/shard_map/ppermute | solution.py:21
  203.6 78.6 %all_gather.43 = bf16[262144]{0:T(1024)(128)(2,1)S(1)} all-gather(bf16[8192]{0:T(1024)(128)(2,1)S(1)} %copy-done.35), channel_id=1, replica_groups=mesh['dp'=4,'ctx'=8] {'dp','ctx'}, dimensions={0}, use_global_device_ids=true | all-gather | bytes 540672 | tf_op jit(solution)/shard_map/all_gather | solution.py:152
  293.9 6.6 copy.104
  306.2 276.0 %conditional.3 = (f32[8,512]{1,0:T(8,128)}, f32[8,512]{1,0:T(8,128)}, f32[8,512,64]{1,2,0:T(8,128)}, f32[8,512]{1,0:T(8,128)S(1)}) conditional(s32[]{:T(128)} %convert_element_type.146, () %tuple.143, (s32[]{:T(128)}, bf16[512,512]{1,0:T(8,128)(2,1)S(1)}, s32[]{:T(128)}, s32[]{:T(128)}, bf16[512,512]{1,0:T(8,128)(2,1)S(1)}, ...), branch_computations={%region_3.4_spmd, %region_4.9_spmd.clone.clone} | conditional | flops 283410048 | bytes 96266384 | solution.py:225
  337.9 243.5 %while.59 = (s32[]{:T(128)}, f32[8,512]{1,0:T(8,128)}, f32[8,512]{1,0:T(8,128)}, f32[8,512,64]{1,2,0:T(8,128)}, s32[16]{0:T(128)S(1)}, /*index=5*/s32[512]{0:T(5...) while((s32[]{:T(128)}, f32[8,512]{1,0:T(8,128)}, ...), condition=%wide.region_8.8_spmd.clone, body=%wide.region_5.7_spmd.clone.sunk | while | flops 283408896 | bytes 33311440 | solution.py:219
  585.5 11.6 multiply_convert_fusion.1
  627.6 199.8 %conditional.4 = (f32[8,512,64]{1,2,0:T(8,128)}) conditional(s32[]{:T(128)} %convert_element_type.146, () %tuple.145, (bf16[4096,512]{1,0:T(8,128)(2,1)}, s32[512]{0:T(512)S(1)}, pred[512]{0:T(512)(128)(4,1)S(1)}, bf16[512,8,64]{0,2,1:T(8,128)(2,1)S(1)}, f32[8,512]{1,0:T(8,128)S(1)}, /*index=5*/bf16[16,256,8,64]{1,0,3,2:T(8,128)(2,1)}, ...), branch_computations={%region_14.15_spmd, %region_15.18_spmd} | conditional | flops 410267136 | bytes 37807500 | solution.py:314
  627.6 11.2 reshape.742
  638.9 9.1 copy.97
  648.0 5.7 copy.118
  653.7 173.7 %while.60 = (s32[]{:T(128)}, f32[8,512,64]{1,2,0:T(8,128)}, s32[16]{0:T(128)S(1)}, s32[512]{0:T(512)S(1)}, s32[512,1]{0,1:T(1,128)S(1)}, /*index=5*/s32[512,1]{0...) while((s32[]{:T(128)}, f32[8,512,64]{1,2,0:T(8,128)}, ...), condition=%wide.region_17.17_spmd.clone, body=%wide.region_16.16_spmd.clone.sunk | while | flops 410266112 | bytes 12635323 | solution.py:308
  827.4 30.8 %all_gather.49 = f32[4096,16]{0,1:T(8,128)S(1)} all-gather(f32[512,16]{0,1:T(8,128)S(1)} %pad_maximum_fusion.3), channel_id=1, replica_groups=mesh['dp'=4,'ctx'=8] {'ctx'}, dimensions={0}, use_global_device_ids=true | all-gather | bytes 294912 | tf_op jit(solution)/shard_map/all_gather | solution.py:279
  861.0 303.2 %conditional.5 = (f32[8,512,64]{1,2,0:T(8,128)}, bf16[8,512,64]{1,2,0:T(8,128)(2,1)}, f32[512]{0:T(512)S(1)}) conditional(s32[]{:T(128)} %convert_element_type.166, () %tuple.147, (bf16[4096,512]{1,0:T(8,128)(2,1)}, bf16[4096,512]{0,1:T(8,128)(2,1)}, bf16[512,512]{1,0:T(8,128)(2,1)S(1)}, bf16[512,512]{1,0:T(8,128)(2,1)}, s32[512]{0:T(512)S(1)}, ...), branch_computations={%region_18.19_spmd, %region_19.23_spmd} | conditional | flops 549995520 | bytes 58681376 | solution.py:351
  861.6 11.4 reshape.743
  873.0 9.1 copy.98
  893.0 270.3 %while.61 = (s32[]{:T(128)}, f32[8,512,64]{1,2,0:T(8,128)}, f32[8,512,64]{1,2,0:T(8,128)S(1)}, s32[512]{0:T(512)S(1)}, s32[16]{0:T(128)}, /*index=5*/s32[1,512]{...) while((s32[]{:T(128)}, f32[8,512,64]{1,2,0:T(8,128)}, ...), condition=%wide.region_22.22_spmd.clone, body=%wide.region_20.21_spmd.clone.sunk | while | flops 549208576 | bytes 19347220 | solution.py:345
  920.8 5.7 fusion.196
  937.7 5.7 fusion.196
  954.6 5.7 fusion.196
  971.5 5.7 fusion.196
  988.4 5.7 fusion.196
  1022.2 5.7 fusion.196
  1056.1 5.7 fusion.196
  1089.9 5.7 fusion.196
  1123.7 5.7 fusion.196
  1157.6 5.7 fusion.196
  1189.7 39.1 %all-reduce.7 = (f32[4096]{0:T(1024)S(1)}, f32[2048]{0:T(1024)S(1)}) all-reduce(f32[4096]{0:T(1024)S(1)} %constant_dynamic-update-slice_fusion.7, f32[2048]{0:T(1024)S(1)} %pad_maximum_fusion.4), channel_id=6, replica_groups=mesh['dp'=4,'ctx'=8] {'dp','ctx'}, use_global_device_ids=true, to_apply=%region_34.35.clone | all-reduce | flops 6144 | bytes 49152
  1230.0 176.2 %all-reduce.11.cloned.1.call-done = (f32[786432]{0:T(1024)}, f32[262144]{0:T(1024)}, f32[1048576]{0:T(1024)}, f32[1048576]{0:T(1024)}) async-done(((f32[786432]{0:T(1024)}, f32[262144]{0:T(1024)}, f32[1048576]{0:T(1024)}, f32[1048576]{0:T(1024)}), (f32[786432]{0:T(1024)}, f32[262144]{0:T(1024)}, f32[1048576]{0:T(1024)}, f32[1048576]{0:T(1024)})) %all-reduce.11.cloned.1.call-update) | async-done | bytes 12582928
  (720 shorter events, 760.3 us)
Async XLA Ops:
  7.2 113.8 %all-gather.9.cloned.1.call-start = ((), (), s32[]{:S(2)}) async-start(), calls=%async_computation | async-start | bytes 1622016 | tf_op jit(solution)/shard_map/all_gather | solution.py:151
  7.9 277.4 %all-gather.13.cloned.1.call-start = ((), (), s32[]{:S(2)}) async-start(), calls=%async_computation.2 | async-start | bytes 2162688 | tf_op jit(solution)/shard_map/all_gather | solution.py:153
  8.7 280.9 %all-gather.15.cloned.1.call-start = ((), (), s32[]{:S(2)}) async-start(), calls=%async_computation.3 | async-start | bytes 2162688 | tf_op jit(solution)/shard_map/all_gather | solution.py:154
  9.4 284.5 %all-gather.11.cloned.1.call-start = ((), (), s32[]{:S(2)}) async-start(), calls=%async_computation.1 | async-start | bytes 4718592 | tf_op jit(solution)/shard_map/all_gather | solution.py:192
  119.5 5.8 copy-start.24
  125.4 78.2 %copy-start.35 = (bf16[8192]{0:T(1024)(128)(2,1)S(1)}, bf16[8192]{0:T(1024)(128)(2,1)}, u32[]{:S(2)}) copy-start(bf16[8192]{0:T(1024)(128)(2,1)} %param.24) | copy-start | bytes 49156
  125.4 157.9 %copy-start.18 = (bf16[1,512,512]{2,1,0:T(8,128)(2,1)S(1)}, bf16[1,512,512]{2,1,0:T(8,128)(2,1)}, u32[]{:S(2)}) copy-start(bf16[1,512,512]{2,1,0:T(8,128)(2,1)} %param.29) | copy-start | bytes 1572868
  128.4 156.7 %copy-start.9 = (bf16[512,512]{1,0:T(8,128)(2,1)S(1)}, bf16[512,512]{1,0:T(8,128)(2,1)}, u32[]{:S(2)}) copy-start(bf16[512,512]{1,0:T(8,128)(2,1)} %get-tuple-element.1944) | copy-start | bytes 1572868
  128.4 499.2 %all-gather.17.cloned.1.call-start = ((), (), s32[]{:S(2)}) async-start(), calls=%async_computation.4 | async-start | bytes 4718592 | tf_op jit(solution)/shard_map/all_gather | solution.py:282
  130.6 730.3 %all-gather.19.cloned.1.call-start = ((), (), s32[]{:S(2)}) async-start(), calls=%async_computation.5 | async-start | bytes 4718592 | tf_op jit(solution)/shard_map/all_gather | solution.py:316
  130.7 17.7 %collective-permute-start = (bf16[512,512]{1,0:T(8,128)(2,1)}, bf16[512,512]{1,0:T(8,128)(2,1)S(1)}, u32[]{:S(2)}, u32[]{:S(2)}) collective-permute-start(bf16[512,512]{1,0:T(8,128)(2,1)} %slice.91), channel_id=1, source_target_pairs={{0,1},{1,2},{2,3},{3,4},{4,5},{5,6},{6,7},{7,0},{8,9},{9,10},{10,1... | collective-permute-start | bytes 1572872 | tf_op jit(solution)/shard_map/ppermute | solution.py:21
  130.7 20.1 %collective-permute-start.1 = (bf16[512,512]{1,0:T(8,128)(2,1)}, bf16[512,512]{1,0:T(8,128)(2,1)S(1)}, u32[]{:S(2)}, u32[]{:S(2)}) collective-permute-start(bf16[512,512]{1,0:T(8,128)(2,1)} %slice.91), channel_id=1, source_target_pairs={{0,7},{1,0},{2,1},{3,2},{4,3},{5,4},{6,5},{7,6},{8,15},{9,8},{10,9... | collective-permute-start | bytes 1572872 | tf_op jit(solution)/shard_map/ppermute | solution.py:24
  148.3 25.0 %collective-permute-start.2 = (bf16[512,512]{1,0:T(8,128)(2,1)S(1)}, bf16[512,512]{1,0:T(8,128)(2,1)S(1)}, u32[]{:S(2)}, u32[]{:S(2)}) collective-permute-start(bf16[512,512]{1,0:T(8,128)(2,1)S(1)} %collective-permute-done), channel_id=1, source_target_pairs={{0,1},{1,2},{2,3},{3,4},{4,5},{5,6},{6,7},{7,0},{8,9},{9,10},{10,1... | collective-permute-start | bytes 1572872 | tf_op jit(solution)/shard_map/ppermute | solution.py:21
  150.8 50.2 %copy-start.21 = (bf16[512,512]{1,0:T(8,128)(2,1)}, bf16[512,512]{1,0:T(8,128)(2,1)S(1)}, u32[]{:S(2)}) copy-start(bf16[512,512]{1,0:T(8,128)(2,1)S(1)} %collective-permute-done.1) | copy-start | bytes 1572868
  150.8 25.1 %collective-permute-start.3 = (bf16[512,512]{1,0:T(8,128)(2,1)S(1)}, bf16[512,512]{1,0:T(8,128)(2,1)}, u32[]{:S(2)}, u32[]{:S(2)}) collective-permute-start(bf16[512,512]{1,0:T(8,128)(2,1)S(1)} %collective-permute-done.1), channel_id=1, source_target_pairs={{0,7},{1,0},{2,1},{3,2},{4,3},{5,4},{6,5},{7,6},{8,15},{9,8},{10,9... | collective-permute-start | bytes 1572872 | tf_op jit(solution)/shard_map/ppermute | solution.py:24
  173.3 116.2 %copy-start.23 = (bf16[512,512]{1,0:T(8,128)(2,1)}, bf16[512,512]{1,0:T(8,128)(2,1)S(1)}, u32[]{:S(2)}) copy-start(bf16[512,512]{1,0:T(8,128)(2,1)S(1)} %collective-permute-done.2) | copy-start | bytes 1572868
  173.3 27.7 %collective-permute-start.4 = (bf16[512,512]{1,0:T(8,128)(2,1)S(1)}, bf16[512,512]{1,0:T(8,128)(2,1)}, u32[]{:S(2)}, u32[]{:S(2)}) collective-permute-start(bf16[512,512]{1,0:T(8,128)(2,1)S(1)} %collective-permute-done.2), channel_id=1, source_target_pairs={{0,1},{1,2},{2,3},{3,4},{4,5},{5,6},{6,7},{7,0},{8,9},{9,10},{10,1... | collective-permute-start | bytes 1572872 | tf_op jit(solution)/shard_map/ppermute | solution.py:21
  175.8 685.1 %all-gather.21.cloned.1.call-start = ((), (), s32[]{:S(2)}) async-start(), calls=%async_computation.6 | async-start | bytes 4718592 | tf_op jit(solution)/shard_map/all_gather | solution.py:317
  175.9 130.2 %collective-permute-start.5 = (bf16[512,512]{1,0:T(8,128)(2,1)}, bf16[512,512]{1,0:T(8,128)(2,1)}, u32[]{:S(2)}, u32[]{:S(2)}) collective-permute-start(bf16[512,512]{1,0:T(8,128)(2,1)} %collective-permute-done.3), channel_id=1, source_target_pairs={{0,7},{1,0},{2,1},{3,2},{4,3},{5,4},{6,5},{7,6},{8,15},{9,8},{10,9... | collective-permute-start | bytes 1572872 | tf_op jit(solution)/shard_map/ppermute | solution.py:24
  201.0 105.1 %collective-permute-start.6 = (bf16[512,512]{1,0:T(8,128)(2,1)}, bf16[512,512]{1,0:T(8,128)(2,1)}, u32[]{:S(2)}, u32[]{:S(2)}) collective-permute-start(bf16[512,512]{1,0:T(8,128)(2,1)} %collective-permute-done.4), channel_id=1, source_target_pairs={{0,1},{1,2},{2,3},{3,4},{4,5},{5,6},{6,7},{7,0},{8,9},{9,10},{10,1... | collective-permute-start | bytes 1572872 | tf_op jit(solution)/shard_map/ppermute | solution.py:21
  300.5 5.7 copy-start.4
  300.5 5.7 copy-start.22
  356.7 5.6 copy-start
  372.0 5.6 copy-start
  402.6 5.7 copy-start
  585.4 11.6 copy-start.13
  585.5 11.6 copy-start.19
  609.9 7.4 copy-start.32
  614.3 791.9 %all-reduce.11.cloned.1.call-start = ((), (), s32[]{:S(2)}) async-start(), calls=%async_computation.7 | async-start | bytes 25165824
  861.0 12.1 copy-start.5
  1179.4 5.6 copy-start.31
  1179.4 5.7 copy-start.29
  (43 other events, 173.9 us)
Sparse Core Ops, SparseCore 0:
  10.9 57.8 all-gather.8
  71.7 55.3 all-gather.12
  130.2 75.1 all-gather.14
  207.3 78.8 all-gather.10
  288.8 72.7 all-gather.16
  363.5 71.6 all-gather.18
  614.4 74.3 all-gather.20
  1174.1 232.0 all-reduce.10
